TPU v7x, 32 devices: a whole 2x2x4 slice. The times are simulated.
32 devices in a mesh: row: 8 (over y, x, core), col: 4 (over z).
Axes of the slice: x: 2, y: 2, z: 4, core: 2. Of those that a mesh axis runs over, the one named last changes fastest.
Arguments:
- in_map: bfloat16 [128, 128, 256], P('row', 'col'), may hold values from -6 to 6
- tile_w: bfloat16 [3, 3, 256, 256], replicated, may hold values from -0.125 to 0.125
- head_w1: bfloat16 [3, 3, 256, 256], replicated, may hold values from -0.125 to 0.125
- head_w2: bfloat16 [3, 3, 256, 256], replicated, may hold values from -0.125 to 0.125
- box_row: int32 [64, 4], P('row', 'col'), may hold values from 0 to 2
- box_col: int32 [64, 4], P('row', 'col'), may hold values from 0 to 18
- box_target: int32 [64, 4], P('row', 'col'), may hold values from -1 to 15, as said below
- head_cot: bfloat16 [32, 4, 14, 14, 256], P('row', 'col'), may hold values from -6 to 6
Outputs:
- grad_map: bfloat16 [128, 128, 256], P('row', 'col')
- grad_w1: float32 [3, 3, 256, 256], replicated
- grad_w2: float32 [3, 3, 256, 256], replicated
Inputs may be any that keep to these rules, and one draw needn't show every extreme that they name: `box_target`: within each row r of tiles, every head slot d * 4 + h (d below 4, h below 4) is named by exactly one tile slot, and empty slots hold -1. A tile names at most 2 head slots of one device, so it holds at most 8 boxes; in every row of tiles one tile holds 8 boxes, 2 for each device of the row.
All inputs are finite; a program needn't handle non-finite values.
Results may differ from a plain program's by a relative error of at most 0.012.
Values may be sent and summed in bfloat16 or wider, within the bound.
No kernel may reach another device: no remote copies, remote signals or barrier semaphores. Data moves between devices by JAX's collectives and lax.ppermute only.
A program may use at most 64 MiB of HBM per device.

v0:
```python
import math
import jax
import jax.numpy as jnp
from jax import lax
from jax.sharding import PartitionSpec as P

LAYOUT = ("NHWC", "HWIO", "NHWC")


def padded_2(shard, sides, width):
    for axis, dim in sides:
        size, length = (lax.axis_size(axis), shard.shape[dim])
        up = [(i, (i + 1) % size) for i in range(size - 1)]
        down = [(j, i) for i, j in up]
        last = lax.slice_in_dim(shard, length - width, length, axis=dim)
        leading = lax.slice_in_dim(shard, 0, width, axis=dim)
        before = lax.ppermute(last, axis, up)
        after = lax.ppermute(leading, axis, down)
        shard = jnp.concatenate([before, shard, after], axis=dim)
    return shard


def conv_pad(inputs, kernel, margin):
    return lax.conv_general_dilated(
        inputs,
        kernel,
        (1, 1),
        ((margin, margin), (margin, margin)),
        dimension_numbers=LAYOUT,
        preferred_element_type=jnp.float32,
    )


def flip_weights(kernel):
    return jnp.transpose(jnp.flip(kernel, (0, 1)), (0, 1, 3, 2))


def silu_slope(values):
    sigma = jax.nn.sigmoid(values)
    return sigma * (1.0 + values * (1.0 - sigma))


def weight_grad(inputs, deltas):
    channels = inputs.shape[-1]
    box_side = inputs.shape[1]
    padded = jnp.pad(inputs, ((0, 0), (1, 1), (1, 1), (0, 0)))
    flat_delta = deltas.reshape(-1, channels)
    blocks = []
    for shift_y in range(3):
        for shift_x in range(3):
            window = padded[
                :, shift_y : shift_y + box_side, shift_x : shift_x + box_side, :
            ].reshape(-1, channels)
            blocks.append(
                lax.dot_general(
                    window, flat_delta, (((0,), (0,)), ((), ())), preferred_element_type=jnp.float32
                )
            )
    return jnp.stack(blocks).reshape(3, 3, channels, channels)


def pick_rows(table, values):
    flat = values.reshape(values.shape[0], -1)
    return jnp.dot(table, flat, preferred_element_type=jnp.float32).astype(jnp.bfloat16)


def pick_back(table, values):
    return lax.dot_general(
        table, values, (((0,), (0,)), ((), ())), preferred_element_type=jnp.float32
    ).astype(jnp.bfloat16)


def body(in_map, tile_w, head_w1, head_w2, box_row, box_col, box_target, head_cot):
    tile_rows, tile_cols, channels = in_map.shape
    head_count = head_cot.shape[0]
    box_side = head_cot.shape[2]
    slot_count = box_target.shape[0]
    columns = lax.axis_size("col")
    capacity = slot_count // columns
    pair_count = columns * capacity
    padded = padded_2(in_map, (("row", 0), ("col", 1)), 1)
    preact = conv_pad(padded[None], tile_w, 0)[0]
    target = box_target[:, 0]
    occupied = target >= 0
    dest_col = jnp.where(occupied, target // head_count, 0)
    head_slot = jnp.where(occupied, target % head_count, 0)
    slot_ids = jnp.arange(slot_count, dtype=jnp.int32)
    same_dest = (dest_col[:, None] == dest_col[None, :]) & occupied[None, :]
    placing = jnp.sum(same_dest & (slot_ids[None, :] < slot_ids[:, None]), axis=1)
    pair_slot = dest_col * capacity + placing
    pair_ids = jnp.arange(pair_count, dtype=jnp.int32)
    send_map = ((pair_slot[None, :] == pair_ids[:, None]) & occupied[None, :]).astype(jnp.bfloat16)
    head_ids = jnp.arange(head_count, dtype=jnp.int32)
    head_hot = ((head_slot[:, None] == head_ids[None, :]) & occupied[:, None]).astype(jnp.bfloat16)
    pair_head = (
        jnp.dot(send_map, head_hot, preferred_element_type=jnp.float32)
        .astype(jnp.bfloat16)
        .reshape(columns, capacity, head_count)
    )
    top_row = box_row[:, 0]
    left_col = box_col[:, 0]
    zero_index = jnp.zeros((), jnp.int32)
    window = box_side + 2
    windows = jax.vmap(
        lambda y, x: lax.dynamic_slice(padded, (y, x, zero_index), (window, window, channels))
    )(top_row, left_col)
    outgoing = pick_rows(send_map, windows).reshape(columns, capacity, window, window, channels)
    arrived, arrived_head = (
        lax.all_to_all(outgoing, "col", split_axis=0, concat_axis=0, tiled=True),
        lax.all_to_all(pair_head, "col", split_axis=0, concat_axis=0, tiled=True),
    )
    arrived_head = arrived_head.reshape(pair_count, head_count)
    gathered = pick_back(arrived_head, arrived.reshape(pair_count, -1)).reshape(
        head_count, window, window, channels
    )
    box_input = jax.nn.silu(conv_pad(gathered, tile_w, 0)).astype(jnp.bfloat16)
    factor = 1.0 / math.sqrt(lax.axis_size("row") * columns * head_count * box_side * box_side)
    cotangent = head_cot[:, 0]
    pre_one = conv_pad(box_input, head_w1, 1)
    hidden = jax.nn.silu(pre_one).astype(jnp.bfloat16)
    pre_two = conv_pad(hidden, head_w2, 1)
    delta_two = (cotangent.astype(jnp.float32) * silu_slope(pre_two)).astype(jnp.bfloat16)
    second_local = weight_grad(hidden, delta_two)
    delta_one = (conv_pad(delta_two, flip_weights(head_w2), 1) * silu_slope(pre_one)).astype(
        jnp.bfloat16
    )
    box_grads = conv_pad(delta_one, flip_weights(head_w1), 1).astype(jnp.bfloat16)
    sent_back = pick_rows(arrived_head, box_grads).reshape(
        columns, capacity, box_side, box_side, channels
    )
    returned = lax.all_to_all(sent_back, "col", split_axis=0, concat_axis=0, tiled=True)
    slot_grads = pick_back(send_map, returned.reshape(pair_count, -1)).reshape(
        slot_count, box_side, box_side, channels
    )
    first_local = weight_grad(box_input, delta_one)
    first_sum, second_sum = lax.psum((first_local, second_local), ("row", "col"))

    def add_box(slot, running):
        current = lax.dynamic_slice(
            running, (top_row[slot], left_col[slot], zero_index), (box_side, box_side, channels)
        )
        return lax.dynamic_update_slice(
            running,
            current + slot_grads[slot].astype(jnp.float32),
            (top_row[slot], left_col[slot], zero_index),
        )

    box_total = lax.fori_loop(
        0, slot_count, add_box, jnp.zeros((tile_rows, tile_cols, channels), jnp.float32)
    )
    delta_map = (box_total * silu_slope(preact)).astype(jnp.bfloat16)
    delta_rim = padded_2(delta_map, (("row", 0), ("col", 1)), 1)
    grad_map = conv_pad(delta_rim[None], flip_weights(tile_w), 0)[0].astype(jnp.bfloat16)
    return (grad_map, first_sum * factor, second_sum * factor)


def solution(mesh):
    in_specs = (
        P("row", "col", None),
        P(),
        P(),
        P(),
        P("row", "col"),
        P("row", "col"),
        P("row", "col"),
        P("row", "col", None, None, None),
    )
    out_specs = (P("row", "col", None), P(), P())
    return jax.shard_map(body, mesh=mesh, in_specs=in_specs, out_specs=out_specs, check_vma=False)
```

profile of v0, /device:TPU:0, one launch (start us, length us, event | category | flops | bytes accessed | tf_op | source)
XLA Modules:
  0.0 296.8 jit_solution(2329614647910186350)
XLA Ops:
  7.2 0.8 fusion.207
  8.0 1.3 collective-permute-start.1
  9.3 3.0 %collective-permute-start = (bf16[1,32,256]{2,1,0:T(8,128)(2,1)S(1)}, bf16[1,32,256]{2,1,0:T(8,128)(2,1)S(1)}, u32[]{:S(2)}, u32[]{:S(2)}) collective-permute-start(bf16[1,32,256]{2,1,0:T(8,128)(2,1)S(1)} %get-tuple-element.174), channel_id=1, source_target_pairs={{0,4},{4,8},{8,12},{12,16},{16,20},{20,24},{24,28},{1,5},{5,9},{9,... | collective-permute-start | bytes 49160 | tf_op jit(solution)/shard_map/ppermute | solution.py:17
  15.9 1.0 constant_dynamic-update-slice_fusion.1
  16.9 5.0 %collective-permute-start.2 = (bf16[18,1,256]{2,1,0:T(2,128)(2,1)S(1)}, bf16[18,1,256]{2,1,0:T(2,128)(2,1)S(1)}, u32[]{:S(2)}, u32[]{:S(2)}) collective-permute-start(bf16[18,1,256]{2,1,0:T(2,128)(2,1)S(1)} %get-tuple-element.169), channel_id=1, source_target_pairs={{0,1},{1,2},{2,3},{4,5},{5,6},{6,7},{8,9},{9,10},{10,11},{12,13},{... | collective-permute-start | bytes 27656 | tf_op jit(solution)/shard_map/ppermute | solution.py:17
  21.9 1.3 collective-permute-start.3
  23.3 4.3 %collective-permute-done.3 = bf16[18,1,256]{2,1,0:T(2,128)(2,1)S(1)} collective-permute-done((bf16[18,1,256]{2,1,0:T(2,128)(2,1)S(1)}, bf16[18,1,256]{2,1,0:T(2,128)(2,1)S(1)}, u32[]{:S(2)}, u32[]{:S(2)}) %collective-permute-start.3) | collective-permute-done | bytes 9248 | tf_op jit(solution)/shard_map/ppermute | solution.py:18
  27.8 20.0 %while.15 = (s32[]{:T(128)}, bf16[18,34,256]{2,1,0:T(8,128)(2,1)S(1)}, s32[8,3]{0,1:T(4,128)S(1)}, bf16[8,16,16,256]{3,2,1,0:T(8,128)(2,1)}, s32[]{:T(128)}) while((s32[]{:T(128)}, bf16[18,34,256]{2,1,0:T(8,128)(2,1)S(1)}, s32[8,3]{0,1:T(4,128)S(1)}, bf16[8,16,16,256]{3,2,1,0:T(8,128)(2,1)}, s32[]{:T(128)}) %tuple.64), condition=%wide.while_cond, body=%wide.while_body.sunk | while | flops 2 | bytes 263285 | solution.py:105
  28.4 1.9 bitcast_dynamic-update-slice_fusion.2
  30.9 1.9 bitcast_dynamic-update-slice_fusion.2
  33.4 1.9 bitcast_dynamic-update-slice_fusion.2
  35.9 1.9 bitcast_dynamic-update-slice_fusion.2
  38.4 1.9 bitcast_dynamic-update-slice_fusion.2
  40.9 1.9 bitcast_dynamic-update-slice_fusion.2
  43.4 1.9 bitcast_dynamic-update-slice_fusion.2
  45.9 1.9 bitcast_dynamic-update-slice_fusion.2
  47.8 1.8 copy.157
  50.0 1.2 copy.158
  51.2 4.0 %all-to-all-start.1 = ((bf16[4,2,16,16,256]{4,3,2,1,0:T(8,128)(2,1)}), bf16[4,2,16,16,256]{4,3,2,1,0:T(8,128)(2,1)S(1)}, u32[]{:S(2)}, u32[]{:S(2)}) async-start(bf16[4,2,16,16,256]{4,3,2,1,0:T(8,128)(2,1)} %bitcast.140), calls=%async_computation.1 | async-start | bytes 2097152 | tf_op jit(solution)/shard_map/all_to_all | solution.py:109
  56.4 0.9 convolution_select_fusion.3
  57.3 1.1 copy.111
  58.4 22.7 %all-to-all-done.1 = bf16[4,2,16,16,256]{4,3,2,1,0:T(8,128)(2,1)S(1)} async-done(((bf16[4,2,16,16,256]{4,3,2,1,0:T(8,128)(2,1)}), bf16[4,2,16,16,256]{4,3,2,1,0:T(8,128)(2,1)S(1)}, u32[]{:S(2)}, u32[]{:S(2)}) %all-to-all-start.1) | async-done | bytes 1048608 | tf_op jit(solution)/shard_map/all_to_all | solution.py:109
  81.0 3.4 %all-to-all-start = ((bf16[4,2,4]{2,1,0:T(2,128)(2,1)}), bf16[4,2,4]{2,1,0:T(2,128)(2,1)S(1)}, u32[]{:S(2)}, u32[]{:S(2)}) async-start(bf16[4,2,4]{2,1,0:T(2,128)(2,1)} %bitcast.9), calls=%async_computation | async-start | bytes 4096 | tf_op jit(solution)/shard_map/all_to_all | solution.py:110
  84.9 4.8 %all-to-all-done = bf16[4,2,4]{2,1,0:T(2,128)(2,1)S(1)} async-done(((bf16[4,2,4]{2,1,0:T(2,128)(2,1)}), bf16[4,2,4]{2,1,0:T(2,128)(2,1)S(1)}, u32[]{:S(2)}, u32[]{:S(2)}) %all-to-all-start) | async-done | bytes 96 | tf_op jit(solution)/shard_map/all_to_all | solution.py:110
  90.9 1.3 multiply_convert_fusion.1
  93.4 1.2 fusion.43
  94.7 1.1 select_bitcast_fusion.1
  96.4 1.3 add_multiply_fusion
  97.7 0.7 copy.100
  99.1 1.2 fusion.62
  100.3 0.8 copy-done.6
  101.6 2.9 fusion.9
  105.3 0.9 copy_bitcast_fusion.2
  106.2 2.3 copy.120
  108.4 1.2 reshape.164
  109.6 0.8 copy_bitcast_fusion
  110.4 0.9 reshape.174
  111.4 2.5 convolution_convert_fusion.4
  115.5 0.7 reshape.125
  116.3 1.8 copy.105
  118.1 3.5 %all-to-all-start.2 = ((bf16[4,2,14,14,256]{4,1,3,2,0:T(2,128)(2,1)}), bf16[4,2,14,14,256]{4,1,3,2,0:T(2,128)(2,1)S(1)}, u32[]{:S(2)}, u32[]{:S(2)}) async-start(bf16[4,2,14,14,256]{4,1,3,2,0:T(2,128)(2,1)} %copy.105), calls=%async_computation.2 | async-start | bytes 1605632 | tf_op jit(solution)/shard_map/all_to_all | solution.py:131
  121.6 1.4 fusion.28
  128.4 1.0 fusion.19
  129.4 1.0 fusion.18
  130.5 1.1 fusion.17
  131.5 1.0 fusion.16
  132.6 1.0 fusion.15
  134.0 1.3 fusion.14
  135.5 1.1 fusion.13
  136.5 1.1 fusion.12
  137.6 1.1 fusion.11
  138.6 1.8 all-to-all-done.2
  141.9 45.4 %while.14 = (s32[]{:T(128)}, f32[16,32,256]{2,0,1:T(8,128)S(1)}, s32[8]{0:T(128)S(1)}, s32[8]{0:T(128)S(1)}, bf16[8,14,14,256]{3,2,1,0:T(8,128)(2,1)S(1)}, /*index=5*/s32[]{:T(128)}, s32[]{:T(128)}, s32[]{:T(128)}, s32[]{:T(128)}) while((s32[]{:T(128)}, f32[16,32,256]{2,0,1:T(8,128)S(1)}, s32[8]{0:T(128)S(1)}, s32[8]{0:T(128)S(1)}, ...), condition=%wide.region_2.3_spmd, body=%wide.region_1.2_spmd.sunk | while | flops 100360 | bytes 1706193 | solution.py:148
  187.6 1.3 collective-permute-start.4
  188.9 1.3 collective-permute-start.5
  190.2 4.3 %collective-permute-done.5 = bf16[1,32,256]{2,0,1:T(2,128)(2,1)S(1)} collective-permute-done((bf16[1,32,256]{2,0,1:T(2,128)(2,1)S(1)}, bf16[1,32,256]{2,0,1:T(2,128)(2,1)S(1)}, u32[]{:S(2)}, u32[]{:S(2)}) %collective-permute-start.5) | collective-permute-done | bytes 16416 | tf_op jit(solution)/shard_map/ppermute | solution.py:18
  194.6 1.8 collective-permute-start.6
  196.4 1.3 collective-permute-start.7
  197.8 4.2 %collective-permute-done.7 = bf16[18,1,256]{2,0,1:T(8,128)(2,1)S(1)} collective-permute-done((bf16[18,1,256]{2,0,1:T(8,128)(2,1)S(1)}, bf16[18,1,256]{2,0,1:T(8,128)(2,1)S(1)}, u32[]{:S(2)}, u32[]{:S(2)}) %collective-permute-start.7) | collective-permute-done | bytes 9248 | tf_op jit(solution)/shard_map/ppermute | solution.py:18
  202.4 1.0 fusion.10
  203.5 0.8 copy.131
  204.3 80.6 %all-reduce.5.cloned.1.call-done = (f32[3,3,256,256]{3,2,1,0:T(8,128)}, f32[3,3,256,256]{3,2,1,0:T(8,128)}) async-done(((f32[3,3,256,256]{3,2,1,0:T(8,128)}, f32[3,3,256,256]{3,2,1,0:T(8,128)}), (f32[3,3,256,256]{3,2,1,0:T(8,128)}, f32[3,3,256,256]{3,2,1,0:T(8,128)})) %all-reduce.5.cloned.1.call-update) | async-done | bytes 4718608 | tf_op jit(solution)/shard_map/psum | solution.py:136
  284.9 3.4 %broadcast_multiply_fusion.1 = f32[3,3,256,256]{3,2,1,0:T(8,128)} fusion(f32[3,3,256,256]{3,2,1,0:T(8,128)} %get-tuple-element.153), kind=kLoop, calls=%fused_computation.29 | loop fusion | flops 589824 | bytes 4718592 | tf_op jit(solution)/shard_map/mul | solution.py:154
  288.3 1.6 broadcast_multiply_fusion
  (180 shorter events, 39.3 us)
Async XLA Ops:
  7.2 49.2 %copy-start = (bf16[3,3,256,256]{3,2,1,0:T(8,128)(2,1)S(1)}, bf16[3,3,256,256]{3,2,1,0:T(8,128)(2,1)}, u32[]{:S(2)}) copy-start(bf16[3,3,256,256]{3,2,1,0:T(8,128)(2,1)} %param.11) | copy-start | bytes 3538948
  8.0 8.8 %collective-permute-start.1 = (bf16[1,32,256]{2,1,0:T(8,128)(2,1)S(1)}, bf16[1,32,256]{2,1,0:T(8,128)(2,1)S(1)}, u32[]{:S(2)}, u32[]{:S(2)}) collective-permute-start(bf16[1,32,256]{2,1,0:T(8,128)(2,1)S(1)} %get-tuple-element.173), channel_id=1, source_target_pairs={{4,0},{8,4},{12,8},{16,12},{20,16},{24,20},{28,24},{5,1},{9,5},{13... | collective-permute-start | bytes 49160 | tf_op jit(solution)/shard_map/ppermute | solution.py:18
  9.3 6.6 %collective-permute-start = (bf16[1,32,256]{2,1,0:T(8,128)(2,1)S(1)}, bf16[1,32,256]{2,1,0:T(8,128)(2,1)S(1)}, u32[]{:S(2)}, u32[]{:S(2)}) collective-permute-start(bf16[1,32,256]{2,1,0:T(8,128)(2,1)S(1)} %get-tuple-element.174), channel_id=1, source_target_pairs={{0,4},{4,8},{8,12},{12,16},{16,20},{20,24},{24,28},{1,5},{5,9},{9,... | collective-permute-start | bytes 49160 | tf_op jit(solution)/shard_map/ppermute | solution.py:17
  16.9 6.4 %collective-permute-start.2 = (bf16[18,1,256]{2,1,0:T(2,128)(2,1)S(1)}, bf16[18,1,256]{2,1,0:T(2,128)(2,1)S(1)}, u32[]{:S(2)}, u32[]{:S(2)}) collective-permute-start(bf16[18,1,256]{2,1,0:T(2,128)(2,1)S(1)} %get-tuple-element.169), channel_id=1, source_target_pairs={{0,1},{1,2},{2,3},{4,5},{5,6},{6,7},{8,9},{9,10},{10,11},{12,13},{... | collective-permute-start | bytes 27656 | tf_op jit(solution)/shard_map/ppermute | solution.py:17
  21.9 5.7 %collective-permute-start.3 = (bf16[18,1,256]{2,1,0:T(2,128)(2,1)S(1)}, bf16[18,1,256]{2,1,0:T(2,128)(2,1)S(1)}, u32[]{:S(2)}, u32[]{:S(2)}) collective-permute-start(bf16[18,1,256]{2,1,0:T(2,128)(2,1)S(1)} %get-tuple-element.170), channel_id=1, source_target_pairs={{1,0},{2,1},{3,2},{5,4},{6,5},{7,6},{9,8},{10,9},{11,10},{13,12},{... | collective-permute-start | bytes 27656 | tf_op jit(solution)/shard_map/ppermute | solution.py:18
  50.0 5.2 %copy-start.19 = (s32[8,1]{0,1:T(1,128)S(1)}, s32[8,1]{0,1:T(1,128)}, u32[]{:S(2)}) copy-start(s32[8,1]{0,1:T(1,128)} %param.16) | copy-start | bytes 100
  51.2 5.2 %copy-start.20 = (pred[8,5]{0,1:T(8,128)(4,1)S(1)}, pred[8,5]{0,1:T(8,128)(4,1)}, u32[]{:S(2)}) copy-start(pred[8,5]{0,1:T(8,128)(4,1)} %constant.129) | copy-start | bytes 124
  51.2 29.9 %all-to-all-start.1 = ((bf16[4,2,16,16,256]{4,3,2,1,0:T(8,128)(2,1)}), bf16[4,2,16,16,256]{4,3,2,1,0:T(8,128)(2,1)S(1)}, u32[]{:S(2)}, u32[]{:S(2)}) async-start(bf16[4,2,16,16,256]{4,3,2,1,0:T(8,128)(2,1)} %bitcast.140), calls=%async_computation.1 | async-start | bytes 2097152 | tf_op jit(solution)/shard_map/all_to_all | solution.py:109
  81.0 8.7 %all-to-all-start = ((bf16[4,2,4]{2,1,0:T(2,128)(2,1)}), bf16[4,2,4]{2,1,0:T(2,128)(2,1)S(1)}, u32[]{:S(2)}, u32[]{:S(2)}) async-start(bf16[4,2,4]{2,1,0:T(2,128)(2,1)} %bitcast.9), calls=%async_computation | async-start | bytes 4096 | tf_op jit(solution)/shard_map/all_to_all | solution.py:110
  90.2 0.7 copy-start.14
  92.2 1.3 copy-start.18
  94.7 1.2 copy-start.8
  94.7 1.8 copy-start.17
  100.3 0.8 copy-start.6
  105.3 6.1 %copy-start.4 = (bf16[14,4,16,256]{3,2,1,0:T(8,128)(2,1)}, bf16[14,4,16,256]{3,2,1,0:T(8,128)(2,1)S(1)}, u32[]{:S(2)}) copy-start(bf16[14,4,16,256]{3,2,1,0:T(8,128)(2,1)S(1)} %reshape.159) | copy-start | bytes 1376260
  116.3 5.3 %copy-start.10 = (bf16[4,14,14,256]{3,2,1,0:T(8,128)(2,1)S(1)}, bf16[4,14,14,256]{3,2,1,0:T(8,128)(2,1)}, u32[]{:S(2)}) copy-start(bf16[4,14,14,256]{3,2,1,0:T(8,128)(2,1)} %copy_bitcast_fusion.2) | copy-start | bytes 1204228
  118.1 22.3 %all-to-all-start.2 = ((bf16[4,2,14,14,256]{4,1,3,2,0:T(2,128)(2,1)}), bf16[4,2,14,14,256]{4,1,3,2,0:T(2,128)(2,1)S(1)}, u32[]{:S(2)}, u32[]{:S(2)}) async-start(bf16[4,2,14,14,256]{4,1,3,2,0:T(2,128)(2,1)} %copy.105), calls=%async_computation.2 | async-start | bytes 1605632 | tf_op jit(solution)/shard_map/all_to_all | solution.py:131
  121.6 1.5 copy-start.12
  121.6 163.3 %all-reduce.5.cloned.1.call-start = ((), (), s32[]{:S(2)}) async-start(), calls=%async_computation.3 | async-start | bytes 9437184 | tf_op jit(solution)/shard_map/psum | solution.py:136
  123.4 1.0 copy-start.13
  124.5 1.0 copy-start.5
  126.2 1.0 copy-start.11
  127.2 1.0 copy-start.7
  127.2 1.2 copy-start.9
  134.0 1.5 copy-start.2
  140.6 1.3 copy-start.15
  140.6 1.3 copy-start.16
  141.9 45.5 %copy-start.3 = (f32[16,8,5,256]{3,0,2,1:T(8,128)S(1)}, f32[16,8,5,256]{3,0,2,1:T(8,128)}, u32[]{:S(2)}) copy-start(f32[16,8,5,256]{3,0,2,1:T(8,128)} %copy.111) | copy-start | bytes 1966084
  187.6 2.6 collective-permute-start.4
  188.9 5.6 %collective-permute-start.5 = (bf16[1,32,256]{2,0,1:T(2,128)(2,1)S(1)}, bf16[1,32,256]{2,0,1:T(2,128)(2,1)S(1)}, u32[]{:S(2)}, u32[]{:S(2)}) collective-permute-start(bf16[1,32,256]{2,0,1:T(2,128)(2,1)S(1)} %get-tuple-element.172), channel_id=1, source_target_pairs={{4,0},{8,4},{12,8},{16,12},{20,16},{24,20},{28,24},{5,1},{9,5},{13... | collective-permute-start | bytes 49160 | tf_op jit(solution)/shard_map/ppermute | solution.py:18
  194.6 3.2 %collective-permute-start.6 = (bf16[18,1,256]{2,0,1:T(8,128)(2,1)S(1)}, bf16[18,1,256]{2,0,1:T(8,128)(2,1)S(1)}, u32[]{:S(2)}, u32[]{:S(2)}) collective-permute-start(bf16[18,1,256]{2,0,1:T(8,128)(2,1)S(1)} %get-tuple-element.167), channel_id=1, source_target_pairs={{0,1},{1,2},{2,3},{4,5},{5,6},{6,7},{8,9},{9,10},{10,11},{12,13},{... | collective-permute-start | bytes 27656 | tf_op jit(solution)/shard_map/ppermute | solution.py:17
  196.4 5.6 %collective-permute-start.7 = (bf16[18,1,256]{2,0,1:T(8,128)(2,1)S(1)}, bf16[18,1,256]{2,0,1:T(8,128)(2,1)S(1)}, u32[]{:S(2)}, u32[]{:S(2)}) collective-permute-start(bf16[18,1,256]{2,0,1:T(8,128)(2,1)S(1)} %get-tuple-element.168), channel_id=1, source_target_pairs={{1,0},{2,1},{3,2},{5,4},{6,5},{7,6},{9,8},{10,9},{11,10},{13,12},{... | collective-permute-start | bytes 27656 | tf_op jit(solution)/shard_map/ppermute | solution.py:18
  284.9 3.4 %copy-start.1 = (f32[3,3,256,256]{3,2,1,0:T(8,128)S(1)}, f32[3,3,256,256]{3,2,1,0:T(8,128)}, u32[]{:S(2)}) copy-start(f32[3,3,256,256]{3,2,1,0:T(8,128)} %get-tuple-element.154) | copy-start | bytes 7077892
Sparse Core Ops, SparseCore 0:
  138.8 146.0 all-reduce.4
where the time goes:
time: 298 us; the launch traced here: 297 us
  waiting for transfers between devices  123 us (41%)
  local copies, waits for them, and re-layouts  60.4 us (20%)
  loops' own time  31.5 us (11%)
  starting transfers between devices  27.2 us (9%)
  matrix products  27.2 us (9%)
  between operations  14.9 us (5%)
  other arithmetic  12.8 us (4%)
    psum x1, waiting for transfers between devices, body(): lax.psum((first_local, second_local), ('row', 'col'))  80.6 us
    another operation x1, loops' own time, body(): lax.fori_loop(0, slot_count, add_box, jnp.zeros((tile_rows, tile_cols, ch...  31.5 us
    all_to_all x1, waiting for transfers between devices, body(): lax.all_to_all(outgoing, 'col', split_axis=0, concat_axis=0, tiled=True)  22.7 us
    gather x24, local copies, waits for them, and re-layouts  19.9 us
    dot_general x18, matrix products, weight_grad(): lax.dot_general(window, flat_delta, (((0,), (0,)), ((), ())), preferred_e...  14 us
    ppermute x4, waiting for transfers between devices, padded_2(): after = lax.ppermute(leading, axis, down)  12.8 us
    ppermute x4, starting transfers between devices, padded_2(): before = lax.ppermute(last, axis, up)  11.1 us
    conv_general_dilated x7, matrix products, conv_pad(): lax.conv_general_dilated(inputs, kernel, (1, 1), ((margin, margin), (marg...  11.1 us
  transfers between devices with their start and end apart: 12, of which 9 were waited for; matrix products, arithmetic and copies ran while one was open for 13% of the time, Pallas kernels for 0%

commit v1 on v0

--- a/solution.py
+++ b/solution.py
@@ -5,6 +5,11 @@
 from jax.sharding import PartitionSpec as P
 
 LAYOUT = ("NHWC", "HWIO", "NHWC")
+
+
+def by_each_axis(array, inner_axis, outer_axis):
+    partial = lax.psum(array, inner_axis)
+    return lax.psum(partial, outer_axis)
 
 
 def padded_2(shard, sides, width):
@@ -133,7 +138,7 @@
         slot_count, box_side, box_side, channels
     )
     first_local = weight_grad(box_input, delta_one)
-    first_sum, second_sum = lax.psum((first_local, second_local), ("row", "col"))
+    first_sum, second_sum = by_each_axis((first_local, second_local), "col", "row")
 
     def add_box(slot, running):
         current = lax.dynamic_slice(

time: 298 us -> 408 us (1.37)
  waiting for transfers between devices: 123 us -> 242 us
  local copies, waits for them, and re-layouts: 60.4 us -> 50.2 us
    psum x1 -> x2, waiting for transfers between devices: 80.6 us -> 160 us  [the longest x1 133 us: by_each_axis(): partial = lax.psum(array, inner_axis)]
    all_to_all x1, waiting for transfers between devices: 1.77 us -> 40 us  [body(): lax.all_to_all(sent_back, 'col', split_axis=0, concat_axis=0, tiled=True)]
    gather x24, local copies, waits for them, and re-layouts: 19.9 us -> 15.5 us
    unnamed x49 -> x55, local copies, waits for them, and re-layouts: 9.91 us -> 9.38 us
  transfers between devices with their start and end apart: 12 -> 13, of which waited for: 9 -> 10; matrix products, arithmetic and copies ran while one was open for 13% -> 8% of each run, Pallas kernels for 0% -> 0%
where the time goes in v1:
time: 408 us; the launch traced here: 407 us
  waiting for transfers between devices  242 us (59%)
  local copies, waits for them, and re-layouts  50.2 us (12%)
  loops' own time  31.6 us (8%)
  matrix products  27.9 us (7%)
  starting transfers between devices  27.1 us (7%)
  between operations  14.9 us (4%)
  other arithmetic  12.7 us (3%)
    psum x1, waiting for transfers between devices, by_each_axis(): partial = lax.psum(array, inner_axis)  133 us
    all_to_all x1, waiting for transfers between devices, body(): lax.all_to_all(sent_back, 'col', split_axis=0, concat_axis=0, tiled=True)  40 us
    another operation x1, loops' own time, body(): lax.fori_loop(0, slot_count, add_box, jnp.zeros((tile_rows, tile_cols, ch...  31.5 us
    psum x1, waiting for transfers between devices, by_each_axis(): return lax.psum(partial, outer_axis)  27 us
    all_to_all x1, waiting for transfers between devices, body(): lax.all_to_all(outgoing, 'col', split_axis=0, concat_axis=0, tiled=True)  24.9 us
    gather x24, local copies, waits for them, and re-layouts  15.5 us
    dot_general x18, matrix products, weight_grad(): lax.dot_general(window, flat_delta, (((0,), (0,)), ((), ())), preferred_e...  13.1 us
    conv_general_dilated x7, matrix products, conv_pad(): lax.conv_general_dilated(inputs, kernel, (1, 1), ((margin, margin), (marg...  12.2 us
  transfers between devices with their start and end apart: 13, of which 10 were waited for; matrix products, arithmetic and copies ran while one was open for 8% of the time, Pallas kernels for 0%

profile of v1, /device:TPU:0, one launch (start us, length us, event | category | flops | bytes accessed | tf_op | source)
XLA Modules:
  0.0 406.7 jit_solution(16923372060400342681)
XLA Ops:
  7.2 0.8 fusion.207
  8.0 1.3 collective-permute-start.1
  9.3 3.0 collective-permute-start
  14.3 0.7 compare_select_fusion
  15.2 0.7 multiply_add_fusion
  15.9 1.0 constant_dynamic-update-slice_fusion.1
  16.9 5.0 %collective-permute-start.2 = (bf16[18,1,256]{2,1,0:T(2,128)(2,1)S(1)}, bf16[18,1,256]{2,1,0:T(2,128)(2,1)S(1)}, u32[]{:S(2)}, u32[]{:S(2)}) collective-permute-start(bf16[18,1,256]{2,1,0:T(2,128)(2,1)S(1)} %get-tuple-element.171), channel_id=1, source_target_pairs={{0,1},{1,2},{2,3},{4,5},{5,6},{6,7},{8,9},{9,10},{10,11},{12,13},{... | collective-permute-start | bytes 27656 | tf_op jit(solution)/shard_map/ppermute | solution.py:22
  21.9 1.3 collective-permute-start.3
  23.3 4.3 %collective-permute-done.3 = bf16[18,1,256]{2,1,0:T(2,128)(2,1)S(1)} collective-permute-done((bf16[18,1,256]{2,1,0:T(2,128)(2,1)S(1)}, bf16[18,1,256]{2,1,0:T(2,128)(2,1)S(1)}, u32[]{:S(2)}, u32[]{:S(2)}) %collective-permute-start.3) | collective-permute-done | bytes 9248 | tf_op jit(solution)/shard_map/ppermute | solution.py:23
  27.6 0.9 fusion.200
  28.5 15.7 %while.15 = (s32[]{:T(128)}, bf16[18,34,256]{2,1,0:T(8,128)(2,1)S(1)}, s32[8,3]{0,1:T(4,128)S(1)}, bf16[8,16,16,256]{3,2,1,0:T(8,128)(2,1)S(1)}, s32[]{:T(128)}) while((s32[]{:T(128)}, bf16[18,34,256]{2,1,0:T(8,128)(2,1)S(1)}, s32[8,3]{0,1:T(4,128)S(1)}, bf16[8,16,16,256]{3,2,1,0:T(8,128)(2,1)S(1)}, s32[]{:T(128)}) %tuple.64), condition=%wide.while_cond, body=%wide.while_body.sunk | while | flops 2 | bytes 262269 | solution.py:110
  29.1 1.3 bitcast_dynamic-update-slice_fusion.2
  31.1 1.3 bitcast_dynamic-update-slice_fusion.2
  33.0 1.3 bitcast_dynamic-update-slice_fusion.2
  35.0 1.3 bitcast_dynamic-update-slice_fusion.2
  37.0 1.3 bitcast_dynamic-update-slice_fusion.2
  38.9 1.3 bitcast_dynamic-update-slice_fusion.2
  40.9 1.3 bitcast_dynamic-update-slice_fusion.2
  42.8 1.3 bitcast_dynamic-update-slice_fusion.2
  45.2 1.2 copy.158
  46.4 3.9 all-to-all-start.1
  50.6 0.7 copy.96
  51.2 24.9 %all-to-all-done.1 = bf16[4,2,16,16,256]{4,3,2,1,0:T(8,128)(2,1)S(1)} async-done(((bf16[4,2,16,16,256]{4,3,2,1,0:T(8,128)(2,1)}), bf16[4,2,16,16,256]{4,3,2,1,0:T(8,128)(2,1)S(1)}, u32[]{:S(2)}, u32[]{:S(2)}) %all-to-all-start.1) | async-done | bytes 1048608 | tf_op jit(solution)/shard_map/all_to_all | solution.py:114
  76.1 3.2 all-to-all-start
  80.1 4.7 %all-to-all-done = bf16[4,2,4]{2,1,0:T(2,128)(2,1)S(1)} async-done(((bf16[4,2,4]{2,1,0:T(2,128)(2,1)}), bf16[4,2,4]{2,1,0:T(2,128)(2,1)S(1)}, u32[]{:S(2)}, u32[]{:S(2)}) %all-to-all-start) | async-done | bytes 96 | tf_op jit(solution)/shard_map/all_to_all | solution.py:115
  86.0 1.3 multiply_convert_fusion.1
  88.2 2.6 fusion.43
  92.3 0.9 copy_bitcast_fusion
  93.3 2.6 add_multiply_fusion
  95.9 0.7 copy.100
  97.3 1.2 fusion.62
  98.5 0.7 copy-done.9
  99.8 2.6 fusion.9
  102.4 0.8 copy-done.3
  108.8 1.3 fusion.19
  110.3 1.0 fusion.18
  111.4 1.1 fusion.17
  112.4 1.0 fusion.16
  113.5 1.0 fusion.15
  114.5 1.0 fusion.14
  115.5 1.1 fusion.13
  116.6 1.1 fusion.12
  117.6 1.1 fusion.11
  118.7 1.0 copy-done.4
  120.1 1.3 convolution_convert_fusion.4
  122.7 0.7 reshape.125
  123.5 1.7 copy.105
  125.2 3.6 all-to-all-start.2
  129.2 0.9 convolution_select_fusion.3
  130.3 40.0 %all-to-all-done.2 = bf16[4,2,14,14,256]{4,1,3,2,0:T(2,128)(2,1)S(1)} async-done(((bf16[4,2,14,14,256]{4,1,3,2,0:T(2,128)(2,1)}), bf16[4,2,14,14,256]{4,1,3,2,0:T(2,128)(2,1)S(1)}, u32[]{:S(2)}, u32[]{:S(2)}) %all-to-all-start.2) | async-done | bytes 802848 | tf_op jit(solution)/shard_map/all_to_all | solution.py:136
  171.1 1.1 convolution_convert_fusion.2
  172.3 133.2 %all-reduce.9.cloned.1.call-done = (f32[3,3,256,256]{3,2,1,0:T(8,128)}, f32[3,3,256,256]{3,2,1,0:T(8,128)}) async-done(((f32[3,3,256,256]{3,2,1,0:T(8,128)}, f32[3,3,256,256]{3,2,1,0:T(8,128)}), (f32[3,3,256,256]{3,2,1,0:T(8,128)}, f32[3,3,256,256]{3,2,1,0:T(8,128)})) %all-reduce.9.cloned.1.call-update) | async-done | bytes 4718608 | tf_op jit(solution)/shard_map/psum | solution.py:11
  306.2 45.5 %while.14 = (s32[]{:T(128)}, f32[16,32,256]{2,0,1:T(8,128)S(1)}, s32[8]{0:T(128)S(1)}, s32[8]{0:T(128)S(1)}, bf16[8,14,14,256]{3,2,1,0:T(8,128)(2,1)S(1)}, /*index=5*/s32[]{:T(128)}, s32[]{:T(128)}, s32[]{:T(128)}, s32[]{:T(128)}) while((s32[]{:T(128)}, f32[16,32,256]{2,0,1:T(8,128)S(1)}, s32[8]{0:T(128)S(1)}, s32[8]{0:T(128)S(1)}, ...), condition=%wide.region_2.3_spmd, body=%wide.region_1.2_spmd.sunk | while | flops 100360 | bytes 1706193 | solution.py:153
  352.0 1.6 collective-permute-start.4
  353.6 1.3 collective-permute-start.5
  354.9 3.2 collective-permute-done.5
  358.1 1.4 collective-permute-start.6
  359.5 1.3 collective-permute-start.7
  360.9 4.6 %collective-permute-done.7 = bf16[18,1,256]{2,0,1:T(8,128)(2,1)S(1)} collective-permute-done((bf16[18,1,256]{2,0,1:T(8,128)(2,1)S(1)}, bf16[18,1,256]{2,0,1:T(8,128)(2,1)S(1)}, u32[]{:S(2)}, u32[]{:S(2)}) %collective-permute-start.7) | collective-permute-done | bytes 9248 | tf_op jit(solution)/shard_map/ppermute | solution.py:23
  366.0 1.0 fusion.10
  367.1 0.8 copy.131
  367.8 27.0 %all-reduce.7.cloned.1.call-done = (f32[3,3,256,256]{3,2,1,0:T(8,128)}, f32[3,3,256,256]{3,2,1,0:T(8,128)}) async-done(((f32[3,3,256,256]{3,2,1,0:T(8,128)}, f32[3,3,256,256]{3,2,1,0:T(8,128)}), (f32[3,3,256,256]{3,2,1,0:T(8,128)}, f32[3,3,256,256]{3,2,1,0:T(8,128)})) %all-reduce.7.cloned.1.call-update) | async-done | bytes 4718608 | tf_op jit(solution)/shard_map/psum | solution.py:12
  394.8 3.4 broadcast_multiply_fusion.1
  398.2 1.6 broadcast_multiply_fusion
  (189 shorter events, 38.1 us)
Async XLA Ops:
  7.2 78.7 %copy-start = (bf16[3,3,256,256]{3,2,1,0:T(8,128)(2,1)S(1)}, bf16[3,3,256,256]{3,2,1,0:T(8,128)(2,1)}, u32[]{:S(2)}) copy-start(bf16[3,3,256,256]{3,2,1,0:T(8,128)(2,1)} %param.11) | copy-start | bytes 3538948
  8.0 8.8 %collective-permute-start.1 = (bf16[1,32,256]{2,1,0:T(8,128)(2,1)S(1)}, bf16[1,32,256]{2,1,0:T(8,128)(2,1)S(1)}, u32[]{:S(2)}, u32[]{:S(2)}) collective-permute-start(bf16[1,32,256]{2,1,0:T(8,128)(2,1)S(1)} %get-tuple-element.175), channel_id=1, source_target_pairs={{4,0},{8,4},{12,8},{16,12},{20,16},{24,20},{28,24},{5,1},{9,5},{13... | collective-permute-start | bytes 49160 | tf_op jit(solution)/shard_map/ppermute | solution.py:23
  9.3 6.6 %collective-permute-start = (bf16[1,32,256]{2,1,0:T(8,128)(2,1)S(1)}, bf16[1,32,256]{2,1,0:T(8,128)(2,1)S(1)}, u32[]{:S(2)}, u32[]{:S(2)}) collective-permute-start(bf16[1,32,256]{2,1,0:T(8,128)(2,1)S(1)} %get-tuple-element.176), channel_id=1, source_target_pairs={{0,4},{4,8},{8,12},{12,16},{16,20},{20,24},{24,28},{1,5},{5,9},{9,... | collective-permute-start | bytes 49160 | tf_op jit(solution)/shard_map/ppermute | solution.py:22
  13.0 37.3 %copy-start.16 = (pred[8]{0:T(512)(128)(4,1)}, pred[8]{0:T(512)(128)(4,1)S(1)}, u32[]{:S(2)}) copy-start(pred[8]{0:T(512)(128)(4,1)S(1)} %bitcast_compare_fusion) | copy-start | bytes 28
  15.9 34.4 %copy-start.17 = (s32[8]{0:T(128)}, s32[8]{0:T(128)S(1)}, u32[]{:S(2)}) copy-start(s32[8]{0:T(128)S(1)} %multiply_add_fusion) | copy-start | bytes 100
  16.9 6.4 %collective-permute-start.2 = (bf16[18,1,256]{2,1,0:T(2,128)(2,1)S(1)}, bf16[18,1,256]{2,1,0:T(2,128)(2,1)S(1)}, u32[]{:S(2)}, u32[]{:S(2)}) collective-permute-start(bf16[18,1,256]{2,1,0:T(2,128)(2,1)S(1)} %get-tuple-element.171), channel_id=1, source_target_pairs={{0,1},{1,2},{2,3},{4,5},{5,6},{6,7},{8,9},{9,10},{10,11},{12,13},{... | collective-permute-start | bytes 27656 | tf_op jit(solution)/shard_map/ppermute | solution.py:22
  21.9 5.7 %collective-permute-start.3 = (bf16[18,1,256]{2,1,0:T(2,128)(2,1)S(1)}, bf16[18,1,256]{2,1,0:T(2,128)(2,1)S(1)}, u32[]{:S(2)}, u32[]{:S(2)}) collective-permute-start(bf16[18,1,256]{2,1,0:T(2,128)(2,1)S(1)} %get-tuple-element.172), channel_id=1, source_target_pairs={{1,0},{2,1},{3,2},{5,4},{6,5},{7,6},{9,8},{10,9},{11,10},{13,12},{... | collective-permute-start | bytes 27656 | tf_op jit(solution)/shard_map/ppermute | solution.py:23
  45.2 5.1 %copy-start.21 = (s32[8,1]{0,1:T(1,128)S(1)}, s32[8,1]{0,1:T(1,128)}, u32[]{:S(2)}) copy-start(s32[8,1]{0,1:T(1,128)} %param.16) | copy-start | bytes 100
  46.4 29.7 %all-to-all-start.1 = ((bf16[4,2,16,16,256]{4,3,2,1,0:T(8,128)(2,1)}), bf16[4,2,16,16,256]{4,3,2,1,0:T(8,128)(2,1)S(1)}, u32[]{:S(2)}, u32[]{:S(2)}) async-start(bf16[4,2,16,16,256]{4,3,2,1,0:T(8,128)(2,1)} %bitcast.140), calls=%async_computation.1 | async-start | bytes 2097152 | tf_op jit(solution)/shard_map/all_to_all | solution.py:114
  76.1 8.7 %all-to-all-start = ((bf16[4,2,4]{2,1,0:T(2,128)(2,1)}), bf16[4,2,4]{2,1,0:T(2,128)(2,1)S(1)}, u32[]{:S(2)}, u32[]{:S(2)}) async-start(bf16[4,2,4]{2,1,0:T(2,128)(2,1)} %bitcast.9), calls=%async_computation | async-start | bytes 4096 | tf_op jit(solution)/shard_map/all_to_all | solution.py:115
  79.4 226.2 %all-reduce.9.cloned.1.call-start = ((), (), s32[]{:S(2)}) async-start(), calls=%async_computation.4 | async-start | bytes 9437184 | tf_op jit(solution)/shard_map/psum | solution.py:11
  85.3 0.7 copy-start.15
  88.0 2.7 copy-start.7
  90.7 0.9 copy-start.12
  92.3 1.0 copy-start.5
  98.5 0.8 copy-start.9
  98.5 1.3 copy-start.13
  102.4 0.8 copy-start.3
  105.0 1.0 copy-start.8
  107.7 1.0 copy-start.10
  107.7 1.1 copy-start.14
  108.8 1.5 copy-start.2
  112.4 1.0 copy-start.6
  118.7 1.0 copy-start.4
  118.7 1.4 copy-start.20
  122.7 6.2 %copy-start.11 = (bf16[18,1,34,256]{3,2,0,1:T(8,128)(2,1)S(1)}, bf16[18,1,34,256]{3,2,0,1:T(8,128)(2,1)}, u32[]{:S(2)}) copy-start(bf16[18,1,34,256]{3,2,0,1:T(8,128)(2,1)} %get-tuple-element.167) | copy-start | bytes 940036
  125.2 3.9 copy-start.22
  125.2 45.1 %all-to-all-start.2 = ((bf16[4,2,14,14,256]{4,1,3,2,0:T(2,128)(2,1)}), bf16[4,2,14,14,256]{4,1,3,2,0:T(2,128)(2,1)S(1)}, u32[]{:S(2)}, u32[]{:S(2)}) async-start(bf16[4,2,14,14,256]{4,1,3,2,0:T(2,128)(2,1)} %copy.105), calls=%async_computation.2 | async-start | bytes 1605632 | tf_op jit(solution)/shard_map/all_to_all | solution.py:136
  128.8 265.9 %all-reduce.7.cloned.1.call-start = ((), (), s32[]{:S(2)}) async-start(), calls=%async_computation.3 | async-start | bytes 9437184 | tf_op jit(solution)/shard_map/psum | solution.py:12
  305.6 0.7 copy-start.18
  305.6 0.7 copy-start.19
  351.7 14.3 %copy-start.23 = (pred[8,5]{0,1:T(8,128)(4,1)S(1)}, pred[8,5]{0,1:T(8,128)(4,1)}, u32[]{:S(2)}) copy-start(pred[8,5]{0,1:T(8,128)(4,1)} %constant.129) | copy-start | bytes 124
  352.0 2.9 collective-permute-start.4
  353.6 4.5 %collective-permute-start.5 = (bf16[1,32,256]{2,0,1:T(2,128)(2,1)S(1)}, bf16[1,32,256]{2,0,1:T(2,128)(2,1)S(1)}, u32[]{:S(2)}, u32[]{:S(2)}) collective-permute-start(bf16[1,32,256]{2,0,1:T(2,128)(2,1)S(1)} %get-tuple-element.174), channel_id=1, source_target_pairs={{4,0},{8,4},{12,8},{16,12},{20,16},{24,20},{28,24},{5,1},{9,5},{13... | collective-permute-start | bytes 49160 | tf_op jit(solution)/shard_map/ppermute | solution.py:23
  358.1 2.8 collective-permute-start.6
  359.5 6.0 %collective-permute-start.7 = (bf16[18,1,256]{2,0,1:T(8,128)(2,1)S(1)}, bf16[18,1,256]{2,0,1:T(8,128)(2,1)S(1)}, u32[]{:S(2)}, u32[]{:S(2)}) collective-permute-start(bf16[18,1,256]{2,0,1:T(8,128)(2,1)S(1)} %get-tuple-element.170), channel_id=1, source_target_pairs={{1,0},{2,1},{3,2},{5,4},{6,5},{7,6},{9,8},{10,9},{11,10},{13,12},{... | collective-permute-start | bytes 27656 | tf_op jit(solution)/shard_map/ppermute | solution.py:23
  394.8 3.4 copy-start.1
Sparse Core Ops, SparseCore 0:
  118.8 186.6 all-reduce.8
  308.9 85.8 all-reduce.6
